TPU v7x, 1024 devices: a whole 8x8x8 slice. The times are simulated.
1024 devices in a mesh: section: 32 (over z, x_lo), dp: 16 (over y, x_hi), tensor: 2 (over core).
Axes of the slice: x: 8 (x_hi: 2, x_lo: 4; x = x_hi * 4 + x_lo), y: 8, z: 8, core: 2. Of those that a mesh axis runs over, the one named last changes fastest.
Arguments:
- tokens: bfloat16 [32, 2048, 4096], P('section', 'dp', 'tensor'), may hold values from -6 to 6
- lengths: int32 [32, 16], P(None, 'dp'), may hold values from 16 to 128, as said below
- w_query: bfloat16 [32, 4096, 256], P('section', None, 'tensor')
- w_key: bfloat16 [32, 4096, 256], P('section', None, 'tensor')
- w_value: bfloat16 [32, 4096, 256], P('section', None, 'tensor'), may hold values from -0.09375 to 0.09375
- w_out: bfloat16 [32, 256, 4096], P('section', 'tensor'), may hold values from -0.375 to 0.375
- w_embed: bfloat16 [4096, 1024], P('tensor'), may hold values from -0.09375 to 0.09375
Outputs:
- penalty_grad: float32 [32, 2048, 1024], P('section', 'dp', 'tensor')
Inputs may be any that keep to these rules, and one draw needn't show every extreme that they name: `lengths`: every length is at least 16; at least one length equals 128.
All inputs are finite; a program needn't handle non-finite values.
Results may differ from a plain program's by a relative error of at most 0.02.
Values may be sent and summed in bfloat16 or wider, within the bound.
A program may use at most 32 MiB of HBM per device.

v0:
```python
import math

import jax
import jax.numpy as jnp
from jax import lax
from jax.sharding import PartitionSpec as P

HD = 128
HOPS = 2


EPSILON = 1e-05


def shifted(value, axis, steps):
    count = lax.axis_size(axis)
    pairs = [(source, (source + steps) % count) for source in range(count)]
    return lax.ppermute(value, axis, pairs)


def attend(features, w_query, w_key, w_value, w_out, live_len):
    seq_rows = features.shape[0]
    local_heads = w_query.shape[1] // HD
    values32 = features.astype(jnp.float32)
    normed = (
        values32 * lax.rsqrt(jnp.mean(values32 * values32, axis=-1, keepdims=True) + EPSILON)
    ).astype(jnp.bfloat16)
    query_rows = jnp.dot(normed, w_query, preferred_element_type=jnp.float32).astype(jnp.bfloat16)
    key_rows = jnp.dot(normed, w_key, preferred_element_type=jnp.float32).astype(jnp.bfloat16)
    value_rows = jnp.dot(normed, w_value, preferred_element_type=jnp.float32).astype(jnp.bfloat16)
    query_h = query_rows.reshape(seq_rows, local_heads, HD)
    key_h = key_rows.reshape(seq_rows, local_heads, HD)
    value_h = value_rows.reshape(seq_rows, local_heads, HD)
    scores = jnp.einsum("qhd,khd->hqk", query_h, key_h, preferred_element_type=jnp.float32) * (
        1.0 / math.sqrt(HD)
    )
    key_mask = lax.broadcasted_iota(jnp.int32, (1, 1, seq_rows), 2) < live_len
    scores = jnp.where(key_mask, scores, -1e30)
    row_max = jnp.max(scores, axis=-1, keepdims=True)
    exp_scores = jnp.exp(scores - row_max)
    attn_probs = (exp_scores / jnp.sum(exp_scores, axis=-1, keepdims=True)).astype(jnp.bfloat16)
    mixed = jnp.einsum(
        "hqk,khd->qhd", attn_probs, value_h, preferred_element_type=jnp.float32
    ).astype(jnp.bfloat16)
    mixed = mixed.reshape(seq_rows, local_heads * HD)
    return jnp.dot(mixed, w_out, preferred_element_type=jnp.float32)


def shards(tokens, lengths, w_query, w_key, w_value, w_out, w_embed):
    section_idx = lax.axis_index("section")
    section_count = lax.axis_size("section")
    core_idx = lax.axis_index("tensor")
    core_count = lax.axis_size("tensor")
    group_idx = lax.axis_index("dp")
    group_count = lax.axis_size("dp")
    per_section = lengths[:, 0]
    state = tokens[0]
    live_len = per_section[0]
    for hop in range(HOPS):
        if hop > 0:
            state = shifted(state, "section", 1)
        anchor = (section_idx - hop) % section_count
        live_len = lax.dynamic_index_in_dim(per_section, anchor, 0, keepdims=False)
        features = lax.all_gather(state, "tensor", axis=1, tiled=True)
        update = attend(features, w_query[0], w_key[0], w_value[0], w_out[0], live_len)
        summed = lax.psum_scatter(
            update.astype(jnp.bfloat16), "tensor", scatter_dimension=1, tiled=True
        ).astype(jnp.float32)
        state = (state.astype(jnp.float32) + summed).astype(jnp.bfloat16)
    seq_rows = state.shape[0]
    embed_part = jnp.dot(state, w_embed, preferred_element_type=jnp.float32)
    embed = lax.psum(embed_part.astype(jnp.bfloat16), "tensor")
    row_live = lax.broadcasted_iota(jnp.int32, (seq_rows, 1), 0) < live_len
    masked = jnp.where(row_live, embed, jnp.zeros_like(embed))
    embed_cols = masked.shape[1]
    half_cols = embed_cols // core_count
    col_start = core_idx * half_cols
    own_cols = lax.dynamic_slice_in_dim(masked, col_start, half_cols, 1)
    moment_part = lax.dot_general(
        masked, own_cols, (((0,), (0,)), ((), ())), preferred_element_type=jnp.float32
    ) / float(seq_rows * group_count)
    moment_block = lax.psum_scatter(
        moment_part.astype(jnp.bfloat16), "dp", scatter_dimension=0, tiled=True
    ).astype(jnp.float32)
    block_rows = moment_block.shape[0]
    row_ids = group_idx * block_rows + lax.broadcasted_iota(jnp.int32, (block_rows, half_cols), 0)
    col_ids = col_start + lax.broadcasted_iota(jnp.int32, (block_rows, half_cols), 1)
    penalty_rows = (moment_block - (row_ids == col_ids).astype(jnp.float32)).astype(jnp.bfloat16)
    result = jnp.dot(
        masked,
        lax.all_gather(penalty_rows, "dp", axis=0, tiled=True),
        preferred_element_type=jnp.float32,
    )
    return result[None]


def solution(mesh):
    return jax.shard_map(
        shards,
        mesh=mesh,
        in_specs=(
            P("section", "dp", "tensor"),
            P(None, "dp"),
            P("section", None, "tensor"),
            P("section", None, "tensor"),
            P("section", None, "tensor"),
            P("section", "tensor", None),
            P("tensor", None),
        ),
        out_specs=P("section", "dp", "tensor"),
        check_vma=False,
    )
```

profile of v0, /device:TPU:1, one launch (start us, length us, event | category | flops | bytes accessed | tf_op | source)
XLA Modules:
  0.0 524.6 jit_solution(16110219197300919816)
XLA Ops:
  6.5 0.7 all-gather.9.cloned.1.call-update
  7.3 1.4 constant_dynamic-slice_fusion.1
  8.7 0.7 iota_compare_fusion
  9.4 35.4 %all-gather.9.cloned.1.call-done = bf16[1,128,4096]{2,1,0:T(8,128)(2,1)} async-done(((bf16[1,128,2048]{2,1,0:T(8,128)(2,1)}), bf16[1,128,4096]{2,1,0:T(8,128)(2,1)}) %all-gather.9.cloned.1.call-update) | async-done | bytes 1048592 | tf_op jit(solution)/shard_map/all_gather | solution.py:64
  44.9 1.6 fusion.2
  46.5 2.0 convolution_convert_fusion.8
  48.5 0.6 fusion.39
  49.2 1.9 fusion.6
  51.1 1.4 convolution_convert_fusion.1
  52.6 21.2 %reduce-scatter.4.cloned.1.call-done = bf16[128,2048]{1,0:T(8,128)(2,1)} async-done(((bf16[128,4096]{1,0:T(8,128)(2,1)}), bf16[128,2048]{1,0:T(8,128)(2,1)}) %reduce-scatter.4.cloned.1.call-update) | async-done | bytes 524304 | tf_op jit(solution)/shard_map/reduce_scatter | solution.py:66
  73.8 1.2 fusion.8
  75.0 1.9 collective-permute-start
  76.9 17.5 %collective-permute-done = bf16[128,2048]{1,0:T(8,128)(2,1)S(1)} collective-permute-done((bf16[128,2048]{1,0:T(8,128)(2,1)S(1)}, bf16[128,2048]{1,0:T(8,128)(2,1)S(1)}, u32[]{:S(2)}, u32[]{:S(2)}) %collective-permute-start) | collective-permute-done | bytes 524320 | tf_op jit(solution)/shard_map/ppermute | solution.py:18
  94.4 0.8 copy-done.2
  95.3 0.7 iota_compare_fusion.1
  96.0 21.6 %all-gather.5.cloned.1.call-done = bf16[128,4096]{1,0:T(8,128)(2,1)} async-done(((bf16[128,2048]{1,0:T(8,128)(2,1)}), bf16[128,4096]{1,0:T(8,128)(2,1)}) %all-gather.5.cloned.1.call-update) | async-done | bytes 1048592 | tf_op jit(solution)/shard_map/all_gather | solution.py:64
  117.6 1.6 fusion
  119.2 1.7 convolution_convert_fusion.4
  121.0 1.9 fusion.44
  123.0 0.7 fusion.7
  123.7 1.4 convolution_convert_fusion
  125.1 0.0 all-reduce.2.cloned.1.call-start
  125.2 21.2 %reduce-scatter.6.cloned.1.call-done = bf16[128,2048]{1,0:T(8,128)(2,1)} async-done(((bf16[128,4096]{1,0:T(8,128)(2,1)}), bf16[128,2048]{1,0:T(8,128)(2,1)}) %reduce-scatter.6.cloned.1.call-update) | async-done | bytes 524304 | tf_op jit(solution)/shard_map/reduce_scatter | solution.py:66
  146.4 3.8 convolution_convert_fusion.2
  150.2 0.0 reduce-scatter.8.cloned.1.call-start
  150.2 42.5 %all-reduce.2.cloned.1.call-done = bf16[128,1024]{1,0:T(8,128)(2,1)} async-done(((bf16[128,1024]{1,0:T(8,128)(2,1)}), bf16[128,1024]{1,0:T(8,128)(2,1)}) %all-reduce.2.cloned.1.call-update) | async-done | bytes 262160 | tf_op jit(solution)/shard_map/psum | solution.py:72
  192.7 1.0 broadcast_select_fusion
  193.8 1.4 multiply_convert_fusion
  195.3 224.2 %reduce-scatter.8.cloned.1.call-done = bf16[64,512]{1,0:T(8,128)(2,1)} async-done(((bf16[1024,512]{1,0:T(8,128)(2,1)}), bf16[64,512]{1,0:T(8,128)(2,1)}) %reduce-scatter.8.cloned.1.call-update) | async-done | bytes 65552 | tf_op jit(solution)/shard_map/reduce_scatter | solution.py:82
  419.5 1.6 subtract_convert_fusion
  421.1 94.4 %all-gather.7.cloned.1.call-done = bf16[1024,512]{1,0:T(8,128)(2,1)} async-done(((bf16[64,512]{1,0:T(8,128)(2,1)}), bf16[1024,512]{1,0:T(8,128)(2,1)}) %all-gather.7.cloned.1.call-update) | async-done | bytes 1048592 | tf_op jit(solution)/shard_map/all_gather | solution.py:91
  515.5 2.2 convolution_bitcast_fusion
  (34 shorter events, 0.4 us)
Async XLA Ops:
  6.5 44.6 %copy-start = (bf16[1,128,4096]{2,1,0:T(8,128)(2,1)S(1)}, bf16[1,128,4096]{2,1,0:T(8,128)(2,1)}, u32[]{:S(2)}) copy-start(bf16[1,128,4096]{2,1,0:T(8,128)(2,1)} %param.12) | copy-start | bytes 3145732
  6.5 42.0 %copy-start.7 = (bf16[1,4096,128]{2,1,0:T(8,128)(2,1)S(1)}, bf16[1,4096,128]{2,1,0:T(8,128)(2,1)}, u32[]{:S(2)}) copy-start(bf16[1,4096,128]{2,1,0:T(8,128)(2,1)} %param.9) | copy-start | bytes 3145732
  6.5 38.3 %all-gather.9.cloned.1.call-start = ((), (), s32[]{:S(2)}) async-start(), calls=%async_computation.9 | async-start | bytes 1572864 | tf_op jit(solution)/shard_map/all_gather | solution.py:64
  7.3 66.6 %reduce-scatter.4.cloned.1.call-start = ((), (), s32[]{:S(2)}) async-start(), calls=%async_computation.3 | async-start | bytes 1572864 | tf_op jit(solution)/shard_map/reduce_scatter | solution.py:66
  44.9 3.7 copy-start.4
  51.1 22.7 %copy-start.1 = (bf16[1,128,2048]{2,1,0:T(8,128)(2,1)S(1)}, bf16[1,128,2048]{2,1,0:T(8,128)(2,1)}, u32[]{:S(2)}) copy-start(bf16[1,128,2048]{2,1,0:T(8,128)(2,1)} %param.7) | copy-start | bytes 1572868
  52.6 66.7 %copy-start.6 = (bf16[1,4096,128]{2,1,0:T(8,128)(2,1)S(1)}, bf16[1,4096,128]{2,1,0:T(8,128)(2,1)}, u32[]{:S(2)}) copy-start(bf16[1,4096,128]{2,1,0:T(8,128)(2,1)} %param.10) | copy-start | bytes 3145732
  52.6 65.0 %all-gather.5.cloned.1.call-start = ((), (), s32[]{:S(2)}) async-start(), calls=%async_computation.4 | async-start | bytes 1572864 | tf_op jit(solution)/shard_map/all_gather | solution.py:64
  75.0 19.4 %collective-permute-start = (bf16[128,2048]{1,0:T(8,128)(2,1)S(1)}, bf16[128,2048]{1,0:T(8,128)(2,1)S(1)}, u32[]{:S(2)}, u32[]{:S(2)}) collective-permute-start(bf16[128,2048]{1,0:T(8,128)(2,1)S(1)} %fusion.8), channel_id=1, source_target_pairs={{0,32},{32,64},{64,96},{96,128},{128,160},{160,192},{192,224},{224... | collective-permute-start | bytes 1572872 | tf_op jit(solution)/shard_map/ppermute | solution.py:18
  94.4 0.8 copy-start.2
  95.3 51.1 %reduce-scatter.6.cloned.1.call-start = ((), (), s32[]{:S(2)}) async-start(), calls=%async_computation.5 | async-start | bytes 1572864 | tf_op jit(solution)/shard_map/reduce_scatter | solution.py:66
  117.6 3.4 copy-start.5
  121.0 2.0 copy-start.8
  123.7 22.7 %copy-start.3 = (bf16[128,2048]{1,0:T(8,128)(2,1)S(1)}, bf16[128,2048]{1,0:T(8,128)(2,1)}, u32[]{:S(2)}) copy-start(bf16[128,2048]{1,0:T(8,128)(2,1)} %copy-done.2) | copy-start | bytes 1572868
  125.1 67.6 %all-reduce.2.cloned.1.call-start = ((), (), s32[]{:S(2)}) async-start(), calls=%async_computation.6 | async-start | bytes 524288 | tf_op jit(solution)/shard_map/psum | solution.py:72
  150.2 269.3 %reduce-scatter.8.cloned.1.call-start = ((), (), s32[]{:S(2)}) async-start(), calls=%async_computation.7 | async-start | bytes 1114112 | tf_op jit(solution)/shard_map/reduce_scatter | solution.py:82
  195.2 320.3 %all-gather.7.cloned.1.call-start = ((), (), s32[]{:S(2)}) async-start(), calls=%async_computation.8 | async-start | bytes 1114112 | tf_op jit(solution)/shard_map/all_gather | solution.py:91
Sparse Core Ops, SparseCore 0:
  10.0 34.8 all-gather.8
  52.7 21.0 reduce-scatter.3
  95.4 22.1 all-gather.4
  125.2 21.0 reduce-scatter.5
  150.3 42.4 all-reduce.1
  198.2 221.2 reduce-scatter.7
  423.8 91.6 all-gather.6
where the time goes:
time: 531 us; the launch traced here: 525 us
  waiting for transfers between devices  479 us (90%)
  matrix products  19.2 us (4%)
  between operations  13.7 us (3%)
  other arithmetic  8.42 us (2%)
    reduce_scatter x1, waiting for transfers between devices, shards(): lax.psum_scatter(moment_part.astype(jnp.bfloat16), 'dp', scatter_dimensio...  224 us
    all_gather x1, waiting for transfers between devices, shards(): lax.all_gather(penalty_rows, 'dp', axis=0, tiled=True)  94.4 us
    all_gather x2, waiting for transfers between devices, shards(): features = lax.all_gather(state, 'tensor', axis=1, tiled=True)  57.1 us
    psum x1, waiting for transfers between devices, shards(): embed = lax.psum(embed_part.astype(jnp.bfloat16), 'tensor')  42.5 us
    reduce_scatter x2, waiting for transfers between devices, shards(): lax.psum_scatter(update.astype(jnp.bfloat16), 'tensor', scatter_dimension...  42.4 us
    ppermute x1, waiting for transfers between devices, shifted(): return lax.ppermute(value, axis, pairs)  17.5 us
  transfers between devices with their start and end apart: 8, of which 8 were waited for; matrix products, arithmetic and copies ran while one was open for 1% of the time, Pallas kernels for 0%

commit v1 on v0

v1 whole, which is shorter than its diff:
```python
import math

import jax
import jax.numpy as jnp
from jax import lax
from jax.experimental import pallas as pl
from jax.experimental.pallas import tpu as pltpu
from jax.sharding import PartitionSpec as P

HD = 128
SEQ = 128
D = 4096
HALF = 2048
E = 1024
EH = 512
CH = 8
CW = HALF // CH
SUB = 2
SROWS = 64 // SUB
SECTIONS = 32
GROUPS = 16
EPSILON = 1e-05
BF = jnp.bfloat16
F32 = jnp.float32

TOK, WOUT, MIX, STATE, RELAY = 0, 1, 2, 4, 4 + CH
EPART, WPART, OUTX, RING = 4 + 2 * CH, 5 + 2 * CH, 6 + 2 * CH, 7 + 2 * CH
REMOTES = RING + 16 * SUB


def dot(a, b):
    return jnp.dot(a, b, preferred_element_type=F32)


def dot_nt(a, b):
    return lax.dot_general(a, b, (((1,), (1,)), ((), ())), preferred_element_type=F32)


def squares(x):
    x32 = x.astype(F32)
    return jnp.sum(x32 * x32, axis=-1, keepdims=True)


def attend(qkv, total_sq, live):
    scale = lax.rsqrt(total_sq * (1.0 / D) + EPSILON)
    q = (qkv[:, :HD] * scale).astype(BF)
    k = (qkv[:, HD : 2 * HD] * scale).astype(BF)
    v = (qkv[:, 2 * HD :] * scale).astype(BF)
    scores = dot_nt(q, k) * (1.0 / math.sqrt(HD))
    positions = lax.broadcasted_iota(jnp.int32, (SEQ, SEQ), 1)
    scores = jnp.where(positions < live, scores, -1e30)
    weights = jnp.exp(scores - jnp.max(scores, axis=-1, keepdims=True))
    total = jnp.sum(weights, axis=-1, keepdims=True)
    return (dot(weights.astype(BF), v) / total).astype(BF)


def kernel(
    tok, lens, wq, wk, wv, wo, wemb, out,
    x1, w, wob, we, sb, x2, mx, es, er, wes, wer, eo, eg, acc, outr,
    lsem, ssem, rsem,
):
    s = lax.axis_index("section")
    g = lax.axis_index("dp")
    c = lax.axis_index("tensor")
    o = 1 - c
    y, xh = g // 2, lax.rem(g, 2)
    nxt = lax.rem(s + 1, SECTIONS)
    prv = lax.rem(s + SECTIONS - 1, SECTIONS)
    pair = (s, g, o)
    after = (nxt, g, c)
    before = (prv, g, c)
    up = (s, lax.rem(y + 1, 8) * 2 + xh, c)
    down = (s, lax.rem(y + 7, 8) * 2 + xh, c)
    across = (s, y * 2 + 1 - xh, c)

    def local(i, src, dst):
        return pltpu.make_async_copy(src, dst, lsem.at[i])

    def remote(i, src, dst, device):
        return pltpu.make_async_remote_copy(
            src_ref=src, dst_ref=dst, send_sem=ssem.at[i], recv_sem=rsem.at[i],
            device_id=device, device_id_type=pl.DeviceIdType.MESH,
        )

    loads = [local(0, tok.at[0], x1.at[c])]
    for h in range(2):
        for j, ref in enumerate((wq, wk, wv)):
            loads.append(local(
                1 + 3 * h + j,
                ref.at[0, h * HALF : (h + 1) * HALF, :],
                w.at[h, :, j * HD : (j + 1) * HD],
            ))
    loads.append(local(7, wo.at[0, :, pl.ds(pl.multiple_of(c * HALF, HALF), HALF)], wob.at[c]))
    loads.append(local(8, wemb, we))
    for copy in loads:
        copy.start()

    barrier = pltpu.get_barrier_semaphore()
    for device in (pair, after, before, up, down, across):
        pl.semaphore_signal(barrier, inc=1, device_id=device, device_id_type=pl.DeviceIdType.MESH)
    pl.semaphore_wait(barrier, 6)

    send_tok = remote(TOK, tok.at[0], x1.at[c], pair)
    send_tok.start()
    send_wo = remote(
        WOUT, wo.at[0, :, pl.ds(pl.multiple_of(o * HALF, HALF), HALF)], wob.at[c], pair
    )
    send_wo.start()
    sends = [send_tok, send_wo]

    for copy in loads[:7]:
        copy.wait()
    own = x1[c]
    qkv = dot(own, w[c])
    total_sq = squares(own)
    send_tok.wait_recv()
    other = x1[o]
    qkv = qkv + dot(other, w[o])
    total_sq = total_sq + squares(other)
    mx[0, c] = attend(qkv, total_sq, lens[s, 0])
    send = remote(MIX, mx.at[0, c], mx.at[0, c], pair)
    send.start()
    sends.append(send)
    loads[7].wait()
    send_wo.wait_recv()
    send.wait_recv()

    mix0, mix1 = mx[0, 0], mx[0, 1]
    shifts = []
    for j in range(CH):
        cols = slice(j * CW, (j + 1) * CW)
        update = dot(mix0, wob[0, :, cols]) + dot(mix1, wob[1, :, cols])
        sb[j] = (x1[c, :, cols].astype(F32) + update).astype(BF)
        send = remote(STATE + j, sb.at[j], x2.at[c, j], after)
        send.start()
        shifts.append(send)
    sends += shifts

    loads[8].wait()
    wes[0] = dot(wob[0], we[...]).astype(BF)
    wes[1] = dot(wob[1], we[...]).astype(BF)
    send_we = remote(WPART, wes, wer, pair)
    send_we.start()
    sends.append(send_we)

    qkv = jnp.zeros((SEQ, 3 * HD), F32)
    total_sq = jnp.zeros((SEQ, 1), F32)
    epart = jnp.zeros((SEQ, E), F32)
    relays = []
    for j in range(CH):
        rows = slice(j * CW, (j + 1) * CW)
        shifts[j].wait_recv()
        relay = remote(RELAY + j, x2.at[c, j], x2.at[c, j], pair)
        relay.start()
        relays.append(relay)
        part = x2[c, j]
        qkv = qkv + dot(part, w[c, rows, :])
        total_sq = total_sq + squares(part)
        epart = epart + dot(part, we[rows, :])
    sends += relays
    es[...] = epart.astype(BF)
    send_e = remote(EPART, es, er, pair)
    send_e.start()
    sends.append(send_e)
    for j in range(CH):
        relays[j].wait_recv()
        part = x2[o, j]
        qkv = qkv + dot(part, w[o, j * CW : (j + 1) * CW, :])
        total_sq = total_sq + squares(part)
    live = lens[prv, 0]
    mx[1, c] = attend(qkv, total_sq, live)
    send = remote(MIX + 1, mx.at[1, c], mx.at[1, c], pair)
    send.start()
    sends.append(send)

    send_we.wait_recv()
    wfull = [(wes[h].astype(F32) + wer[h].astype(F32)).astype(BF) for h in range(2)]
    send_e.wait_recv()
    base = es[...].astype(F32) + er[...].astype(F32)
    send.wait_recv()
    embed = base + dot(mx[1, 0], wfull[0]) + dot(mx[1, 1], wfull[1])
    row_ids = lax.broadcasted_iota(jnp.int32, (SEQ, E), 0)
    eo[...] = jnp.where(row_ids < live, embed, 0.0).astype(BF)
    for q in range(SUB):
        eg[0, q] = eo[pl.ds(pl.multiple_of(c * 64 + q * SROWS, SROWS), SROWS), :]

    def hop(col, source, target, q, device):
        i = RING + (col * 8 + target) * SUB + q
        src = eg.at[source, q] if target == 0 else eg.at[col * 8 + source, q]
        send = remote(i, src, eg.at[col * 8 + target, q], device)
        send.start()
        sends.append(send)
        return send

    arrive = {}

    def launch(col, slot, q):
        plus, minus = (4, 3) if col == 0 else (3, 4)
        if slot < plus:
            arrive[col, slot + 1, q] = hop(col, slot, slot + 1, q, up)
        if slot == 0 or slot > 8 - minus:
            prior = 7 if slot == 0 else slot - 1
            arrive[col, prior, q] = hop(col, slot, prior, q, down)

    def launch_own():
        for q in range(SUB):
            launch(0, 0, q)
        for q in range(SUB):
            arrive[1, 0, q] = hop(1, 0, 0, q, across)

    def take(col, slot):
        for q in range(SUB):
            arrive[col, slot, q].wait_recv()
            if slot == 0 or (slot < 4 if col == 0 else slot < 3) or slot > (5 if col == 0 else 4):
                launch(col, slot, q)

    def contract(slots, first=False):
        rows = jnp.concatenate(
            [eg[slot].reshape(64, E) for slot in slots], axis=0
        )
        gram = dot_nt(eo[...], rows).astype(BF)
        for h in range(2):
            term = dot(gram, rows[:, h * EH : (h + 1) * EH])
            acc[h] = term if first else acc[h] + term

    launch_own()
    take(0, 1)
    take(0, 7)
    take(1, 0)
    contract([0, 1, 7, 8], True)
    take(0, 2)
    take(0, 6)
    take(1, 1)
    take(1, 7)
    contract([2, 6, 9, 15])
    take(0, 3)
    take(0, 5)
    take(1, 2)
    take(1, 6)
    contract([3, 5, 10, 14])
    take(0, 4)
    take(1, 3)
    take(1, 5)
    take(1, 4)
    contract([4, 11, 13, 12])

    send = remote(OUTX, acc.at[o], outr, pair)
    send.start()
    sends.append(send)
    send.wait_recv()
    half = eo[:, pl.ds(pl.multiple_of(c * EH, EH), EH)].astype(F32)
    out[0] = (acc[c] + outr[...]) * (1.0 / (SEQ * GROUPS)) - half
    for send in sends:
        send.wait_send()


def shards(tokens, lengths, w_query, w_key, w_value, w_out, w_embed):
    anywhere = pl.BlockSpec(memory_space=pl.ANY)
    return pl.pallas_call(
        kernel,
        out_shape=jax.ShapeDtypeStruct((1, SEQ, EH), F32),
        in_specs=[anywhere, pl.BlockSpec(memory_space=pltpu.SMEM)] + [anywhere] * 5,
        out_specs=pl.BlockSpec(memory_space=pltpu.VMEM),
        scratch_shapes=[
            pltpu.VMEM((2, SEQ, HALF), BF),
            pltpu.VMEM((2, HALF, 3 * HD), BF),
            pltpu.VMEM((2, HD, HALF), BF),
            pltpu.VMEM((HALF, E), BF),
            pltpu.VMEM((CH, SEQ, CW), BF),
            pltpu.VMEM((2, CH, SEQ, CW), BF),
            pltpu.VMEM((2, 2, SEQ, HD), BF),
            pltpu.VMEM((SEQ, E), BF),
            pltpu.VMEM((SEQ, E), BF),
            pltpu.VMEM((2, HD, E), BF),
            pltpu.VMEM((2, HD, E), BF),
            pltpu.VMEM((SEQ, E), BF),
            pltpu.VMEM((16, SUB, SROWS, E), BF),
            pltpu.VMEM((2, SEQ, EH), F32),
            pltpu.VMEM((SEQ, EH), F32),
            pltpu.SemaphoreType.DMA((9,)),
            pltpu.SemaphoreType.DMA((REMOTES,)),
            pltpu.SemaphoreType.DMA((REMOTES,)),
        ],
        compiler_params=pltpu.CompilerParams(
            collective_id=0, has_side_effects=True, vmem_limit_bytes=60 * 1024 * 1024
        ),
    )(tokens, lengths, w_query, w_key, w_value, w_out, w_embed)


def solution(mesh):
    return jax.shard_map(
        shards,
        mesh=mesh,
        in_specs=(
            P("section", "dp", "tensor"),
            P(None, "dp"),
            P("section", None, "tensor"),
            P("section", None, "tensor"),
            P("section", None, "tensor"),
            P("section", "tensor", None),
            P("tensor", None),
        ),
        out_specs=P("section", "dp", "tensor"),
        check_vma=False,
    )
```

time: 531 us -> 79.8 us (0.15); the launches traced: 525 us -> 79.5 us
  waiting for transfers between devices: 479 us -> 0 us
  Pallas kernels: 0 us -> 76.5 us
  matrix products: 19.2 us -> 0 us
  between operations: 13.7 us -> 0.01 us
  other arithmetic: 8.42 us -> 0 us
    reduce_scatter x3 -> x0, waiting for transfers between devices: 267 us -> none  [the longest x1 224 us: shards(): lax.psum_scatter(moment_part.astype(jnp.bfloat16), 'dp', scatter_dimensio...]
    all_gather x3 -> x0, waiting for transfers between devices: 152 us -> none  [the longest x1 94.4 us: shards(): lax.all_gather(penalty_rows, 'dp', axis=0, tiled=True)]
    pallas_call x0 -> x1, Pallas kernels: none -> 76.5 us  [shards(): pl.pallas_call(kernel, out_shape=jax.ShapeDtypeStruct((1, SEQ, EH), F32),...]
    psum x1 -> x0, waiting for transfers between devices: 42.5 us -> none  [shards(): embed = lax.psum(embed_part.astype(jnp.bfloat16), 'tensor')]
    dot_general x11 -> x0, matrix products: 19.2 us -> none  [the longest x1 3.78 us: shards(): embed_part = jnp.dot(state, w_embed, preferred_element_type=jnp.float32)]
    ppermute x1 -> x0, waiting for transfers between devices: 17.5 us -> none  [shifted(): return lax.ppermute(value, axis, pairs)]
  transfers between devices with their start and end apart: 8 -> 0, of which waited for: 8 -> 0; matrix products, arithmetic and copies ran while one was open for 1% -> 0% of each run, Pallas kernels for 0% -> 0%
where the time goes in v1:
time: 79.8 us; the launch traced here: 79.5 us
  Pallas kernels  76.5 us (96%)
  local copies, waits for them, and re-layouts  3.01 us (4%)
    pallas_call x1, Pallas kernels, shards(): pl.pallas_call(kernel, out_shape=jax.ShapeDtypeStruct((1, SEQ, EH), F32),...  76.5 us
    unnamed x2, local copies, waits for them, and re-layouts  3.01 us

profile of v1, /device:TPU:1, one launch (start us, length us, event | category | flops | bytes accessed | tf_op | source)
XLA Modules:
  0.0 79.5 jit_solution(12054059329916808677)
XLA Ops:
  0.0 1.3 %copy.8.lens = s32[32,1]{1,0:T(8,128)} copy(s32[32,1]{0,1:T(1,128)} %param.8) | data formatting | bytes 256 | tf_op args[1]
  1.3 76.5 %shard_map.73 = f32[1,128,512]{2,1,0:T(8,128)} custom-call(bf16[1,128,2048]{2,1,0:T(8,128)(2,1)} %tok.1, s32[32,1]{1,0:T(8,128)} %copy.8.lens, bf16[1,4096,128]{2,1,0:T(8,128)(2,1)} %wq.1, bf16[1,4096,128]{2,1,0:T(8,128)(2,1)} %wk.1, bf16[1,4096,128]{2,1,0:T(8,128)(2,1)} %wv.1, bf16[1,128,4096]{2,1,0:T(8,128)(2,1)} %wo.1, bf16[2048,1024]{1,0:T(8,128)(2,1)} %wemb.1), custom_call_target="tpu_custom_call" | custom-call | tf_op jit(solution)/shard_map/pallas_call | solution.py:259
  77.9 1.7 %copy.10 = f32[1,128,512]{2,1,0:T(8,128)} copy(f32[1,128,512]{2,1,0:T(8,128)} %shard_map.73) | data formatting | bytes 524288

commit v2 on v1

--- a/solution.py
+++ b/solution.py
@@ -25,7 +25,8 @@
 
 TOK, WOUT, MIX, STATE, RELAY = 0, 1, 2, 4, 4 + CH
 EPART, WPART, OUTX, RING = 4 + 2 * CH, 5 + 2 * CH, 6 + 2 * CH, 7 + 2 * CH
-REMOTES = RING + 16 * SUB
+CROSS = RING + 16 * SUB
+REMOTES = CROSS + SUB
 
 
 def dot(a, b):
@@ -56,7 +57,7 @@
 
 def kernel(
     tok, lens, wq, wk, wv, wo, wemb, out,
-    x1, w, wob, we, sb, x2, mx, es, er, wes, wer, eo, eg, acc, outr,
+    x1, w, wob, we, sb, x2, mx, es, er, wes, wer, eo, eg, cross, acc, outr,
     lsem, ssem, rsem,
 ):
     s = lax.axis_index("section")
@@ -71,7 +72,11 @@
     before = (prv, g, c)
     up = (s, lax.rem(y + 1, 8) * 2 + xh, c)
     down = (s, lax.rem(y + 7, 8) * 2 + xh, c)
-    across = (s, y * 2 + 1 - xh, c)
+    x = xh * 4 + lax.rem(s, 4)
+    x_up, x_down = lax.rem(x + 2, 8), lax.rem(x + 6, 8)
+    z4 = (s // 4) * 4
+    ahead = (z4 + lax.rem(x_up, 4), y * 2 + x_up // 4, c)
+    behind = (z4 + lax.rem(x_down, 4), y * 2 + x_down // 4, c)
 
     def local(i, src, dst):
         return pltpu.make_async_copy(src, dst, lsem.at[i])
@@ -92,13 +97,13 @@
             ))
     loads.append(local(7, wo.at[0, :, pl.ds(pl.multiple_of(c * HALF, HALF), HALF)], wob.at[c]))
     loads.append(local(8, wemb, we))
-    for copy in loads:
+    for copy in loads[:7]:
         copy.start()
 
     barrier = pltpu.get_barrier_semaphore()
-    for device in (pair, after, before, up, down, across):
+    for device in (pair, after, before, up, down, ahead, behind):
         pl.semaphore_signal(barrier, inc=1, device_id=device, device_id_type=pl.DeviceIdType.MESH)
-    pl.semaphore_wait(barrier, 6)
+    pl.semaphore_wait(barrier, 7)
 
     send_tok = remote(TOK, tok.at[0], x1.at[c], pair)
     send_tok.start()
@@ -106,10 +111,12 @@
         WOUT, wo.at[0, :, pl.ds(pl.multiple_of(o * HALF, HALF), HALF)], wob.at[c], pair
     )
     send_wo.start()
+    loads[7].start()
     sends = [send_tok, send_wo]
 
     for copy in loads[:7]:
         copy.wait()
+    loads[8].start()
     own = x1[c]
     qkv = dot(own, w[c])
     total_sq = squares(own)
@@ -117,7 +124,7 @@
     other = x1[o]
     qkv = qkv + dot(other, w[o])
     total_sq = total_sq + squares(other)
-    mx[0, c] = attend(qkv, total_sq, lens[s, 0])
+    mx[0, c] = attend(qkv, total_sq, lens[0, s])
     send = remote(MIX, mx.at[0, c], mx.at[0, c], pair)
     send.start()
     sends.append(send)
@@ -167,7 +174,7 @@
         part = x2[o, j]
         qkv = qkv + dot(part, w[o, j * CW : (j + 1) * CW, :])
         total_sq = total_sq + squares(part)
-    live = lens[prv, 0]
+    live = lens[0, prv]
     mx[1, c] = attend(qkv, total_sq, live)
     send = remote(MIX + 1, mx.at[1, c], mx.at[1, c], pair)
     send.start()
@@ -186,8 +193,7 @@
 
     def hop(col, source, target, q, device):
         i = RING + (col * 8 + target) * SUB + q
-        src = eg.at[source, q] if target == 0 else eg.at[col * 8 + source, q]
-        send = remote(i, src, eg.at[col * 8 + target, q], device)
+        send = remote(i, eg.at[col * 8 + source, q], eg.at[col * 8 + target, q], device)
         send.start()
         sends.append(send)
         return send
@@ -205,8 +211,19 @@
     def launch_own():
         for q in range(SUB):
             launch(0, 0, q)
-        for q in range(SUB):
-            arrive[1, 0, q] = hop(1, 0, 0, q, across)
+        for q, device in enumerate((ahead, behind)):
+            send = remote(CROSS + q, eg.at[0, q], cross.at[q], device)
+            send.start()
+            sends.append(send)
+            arrive["cross", q] = send
+
+    def pass_on():
+        for q, device in enumerate((ahead, behind)):
+            arrive["cross", q].wait_recv()
+            send = remote(RING + 8 * SUB + q, cross.at[q], eg.at[8, q], device)
+            send.start()
+            sends.append(send)
+            arrive[1, 0, q] = send
 
     def take(col, slot):
         for q in range(SUB):
@@ -226,37 +243,39 @@
     launch_own()
     take(0, 1)
     take(0, 7)
-    take(1, 0)
-    contract([0, 1, 7, 8], True)
+    pass_on()
+    contract([0, 1, 7], True)
     take(0, 2)
     take(0, 6)
+    take(0, 3)
+    take(0, 5)
+    contract([2, 6, 3, 5])
+    take(1, 0)
+    take(0, 4)
     take(1, 1)
     take(1, 7)
-    contract([2, 6, 9, 15])
-    take(0, 3)
-    take(0, 5)
+    contract([4, 8, 9, 15])
     take(1, 2)
     take(1, 6)
-    contract([3, 5, 10, 14])
-    take(0, 4)
+    contract([10, 14])
     take(1, 3)
     take(1, 5)
     take(1, 4)
-    contract([4, 11, 13, 12])
+    contract([11, 13, 12])
 
     send = remote(OUTX, acc.at[o], outr, pair)
     send.start()
     sends.append(send)
     send.wait_recv()
     half = eo[:, pl.ds(pl.multiple_of(c * EH, EH), EH)].astype(F32)
-    out[0] = (acc[c] + outr[...]) * (1.0 / (SEQ * GROUPS)) - half
+    out[0] = (acc[c] + outr[...]) - half * float(SEQ * GROUPS)
     for send in sends:
         send.wait_send()
 
 
 def shards(tokens, lengths, w_query, w_key, w_value, w_out, w_embed):
     anywhere = pl.BlockSpec(memory_space=pl.ANY)
-    return pl.pallas_call(
+    total = pl.pallas_call(
         kernel,
         out_shape=jax.ShapeDtypeStruct((1, SEQ, EH), F32),
         in_specs=[anywhere, pl.BlockSpec(memory_space=pltpu.SMEM)] + [anywhere] * 5,
@@ -275,6 +294,7 @@
             pltpu.VMEM((2, HD, E), BF),
             pltpu.VMEM((SEQ, E), BF),
             pltpu.VMEM((16, SUB, SROWS, E), BF),
+            pltpu.VMEM((SUB, SROWS, E), BF),
             pltpu.VMEM((2, SEQ, EH), F32),
             pltpu.VMEM((SEQ, EH), F32),
             pltpu.SemaphoreType.DMA((9,)),
@@ -284,7 +304,8 @@
         compiler_params=pltpu.CompilerParams(
             collective_id=0, has_side_effects=True, vmem_limit_bytes=60 * 1024 * 1024
         ),
-    )(tokens, lengths, w_query, w_key, w_value, w_out, w_embed)
+    )(tokens, lengths.reshape(1, SECTIONS), w_query, w_key, w_value, w_out, w_embed)
+    return total * (1.0 / (SEQ * GROUPS))
 
 
 def solution(mesh):

time: 79.8 us -> 82.9 us (1.039)
  Pallas kernels: 76.5 us -> 81 us
  local copies, waits for them, and re-layouts: 3.01 us -> 0 us
  other arithmetic: 0 us -> 1.67 us
    pallas_call x1, Pallas kernels: 76.5 us -> 81 us  [shards(): pl.pallas_call(kernel, out_shape=jax.ShapeDtypeStruct((1, SEQ, EH), F32),...]
    unnamed x2 -> x0, local copies, waits for them, and re-layouts: 3.01 us -> none
    mul x0 -> x1, other arithmetic: none -> 1.67 us  [shards(): return total * (1.0 / (SEQ * GROUPS))]
where the time goes in v2:
time: 82.9 us; the launch traced here: 82.7 us
  Pallas kernels  81 us (98%)
  other arithmetic  1.67 us (2%)
    pallas_call x1, Pallas kernels, shards(): pl.pallas_call(kernel, out_shape=jax.ShapeDtypeStruct((1, SEQ, EH), F32),...  81 us
    mul x1, other arithmetic, shards(): return total * (1.0 / (SEQ * GROUPS))  1.67 us

profile of v2, /device:TPU:1, one launch (start us, length us, event | category | flops | bytes accessed | tf_op | source)
XLA Modules:
  0.0 82.7 jit_solution(4987936951289240595)
XLA Ops:
  0.0 81.0 %shard_map.73 = f32[1,128,512]{2,1,0:T(8,128)} custom-call(bf16[1,128,2048]{2,1,0:T(8,128)(2,1)} %tok.1, s32[1,32]{1,0:T(1,128)} %bitcast.1, bf16[1,4096,128]{2,1,0:T(8,128)(2,1)} %wq.1, bf16[1,4096,128]{2,1,0:T(8,128)(2,1)} %wk.1, bf16[1,4096,128]{2,1,0:T(8,128)(2,1)} %wv.1, bf16[1,128,4096]{2,1,0:T(8,128)(2,1)} %wo.1, bf16[2048,1024]{1,0:T(8,128)(2,1)} %wemb.1), custom_call_target="tpu_custom_call" | custom-call | tf_op jit(solution)/shard_map/pallas_call | solution.py:278
  81.0 1.7 %broadcast_multiply_fusion = f32[1,128,512]{2,1,0:T(8,128)} fusion(f32[1,128,512]{2,1,0:T(8,128)} %shard_map.73), kind=kLoop, calls=%fused_computation | loop fusion | flops 65536 | bytes 524288 | tf_op jit(solution)/shard_map/mul | solution.py:308

commit v3 on v1

v3 whole, which is shorter than its diff:
```python
import math

import jax
import jax.numpy as jnp
from jax import lax
from jax.experimental import pallas as pl
from jax.experimental.pallas import tpu as pltpu
from jax.sharding import PartitionSpec as P

HD = 128
SEQ = 128
D = 4096
HALF = 2048
E = 1024
EH = 512
CH = 8
CW = HALF // CH
PART = 64
SECTIONS = 32
GROUPS = 16
EPSILON = 1e-05
BF = jnp.bfloat16
F32 = jnp.float32

FIRST = 3
(TOK, WOUT, MIX, EPART, WPART, ESHIP, EPAIR, ECROSS, EXPAIR, ACROSS, PARTNER, OWN, BACK) = (
    0, 1, 2, 4, 5, 6, 7, 8, 9, 10, 11, 12, 13)
STATE = 14
RELAY = STATE + CH
EGAT = RELAY + CH
AGAT = EGAT + 8
REMOTES = AGAT + 8


def dot(a, b):
    return jnp.dot(a, b, preferred_element_type=F32)


def dot_nt(a, b):
    return lax.dot_general(a, b, (((1,), (1,)), ((), ())), preferred_element_type=F32)


def squares(x):
    x32 = x.astype(F32)
    return jnp.sum(x32 * x32, axis=-1, keepdims=True)


def attend(qkv, total_sq, live):
    scale = lax.rsqrt(total_sq * (1.0 / D) + EPSILON)
    q = (qkv[:, :HD] * scale).astype(BF)
    k = (qkv[:, HD : 2 * HD] * scale).astype(BF)
    v = (qkv[:, 2 * HD :] * scale).astype(BF)
    scores = dot_nt(q, k) * (1.0 / math.sqrt(HD))
    positions = lax.broadcasted_iota(jnp.int32, (SEQ, SEQ), 1)
    scores = jnp.where(positions < live, scores, -1e30)
    weights = jnp.exp(scores - jnp.max(scores, axis=-1, keepdims=True))
    total = jnp.sum(weights, axis=-1, keepdims=True)
    return (dot(weights.astype(BF), v) / total).astype(BF)


def kernel(
    tok, lens, wq, wk, wv, wo, wemb, out,
    x1, w, wob, we, sb, x2, mx, es, er, e1s, e1, xe1, eg, ag, xmx, wes, wer, acc, got, back, gotb,
    lsem, ssem, rsem,
):
    s = lax.axis_index("section")
    g = lax.axis_index("dp")
    c = lax.axis_index("tensor")
    o = 1 - c
    y, xh = g // 2, lax.rem(g, 2)
    nxt = lax.rem(s + 1, SECTIONS)
    prv = lax.rem(s + SECTIONS - 1, SECTIONS)
    pair = (s, g, o)
    after = (nxt, g, c)
    before = (prv, g, c)
    across = (s, y * 2 + 1 - xh, c)
    peers = {d: (s, lax.rem(y + d, 8) * 2 + xh, c) for d in (4, 3, 5, 2, 6, 1, 7)}

    def local(i, src, dst):
        return pltpu.make_async_copy(src, dst, lsem.at[i])

    def remote(i, src, dst, device):
        return pltpu.make_async_remote_copy(
            src_ref=src, dst_ref=dst, send_sem=ssem.at[i], recv_sem=rsem.at[i],
            device_id=device, device_id_type=pl.DeviceIdType.MESH,
        )

    loads = [local(0, tok.at[0], x1.at[c])]
    for h in range(2):
        for j, ref in enumerate((wq, wk, wv)):
            loads.append(local(
                1 + 3 * h + j,
                ref.at[0, h * HALF : (h + 1) * HALF, :],
                w.at[h, :, j * HD : (j + 1) * HD],
            ))
    loads.append(local(7, wo.at[0, :, pl.ds(pl.multiple_of(c * HALF, HALF), HALF)], wob.at[c]))
    loads.append(local(8, wemb, we))
    for copy in loads[:7]:
        copy.start()

    barrier = pltpu.get_barrier_semaphore()
    for device in (pair, after, before, across, *peers.values()):
        pl.semaphore_signal(barrier, inc=1, device_id=device, device_id_type=pl.DeviceIdType.MESH)
    pl.semaphore_wait(barrier, 11)

    send_tok = remote(TOK, tok.at[0], x1.at[c], pair)
    send_tok.start()
    send_wo = remote(
        WOUT, wo.at[0, :, pl.ds(pl.multiple_of(o * HALF, HALF), HALF)], wob.at[c], pair
    )
    send_wo.start()
    loads[7].start()
    sends = [send_tok, send_wo]

    for copy in loads[:7]:
        copy.wait()
    loads[8].start()
    own = x1[c]
    qkv = dot(own, w[c])
    total_sq = squares(own)
    send_tok.wait_recv()
    other = x1[o]
    qkv = qkv + dot(other, w[o])
    total_sq = total_sq + squares(other)
    mx[0, c] = attend(qkv, total_sq, lens[0, s])
    send = remote(MIX, mx.at[0, c], mx.at[0, c], pair)
    send.start()
    sends.append(send)
    loads[7].wait()
    send_wo.wait_recv()
    send.wait_recv()

    def start(i, src, dst, device):
        copy = remote(i, src, dst, device)
        copy.start()
        sends.append(copy)
        return copy

    loads[8].wait()
    mix0, mix1 = mx[0, 0], mx[0, 1]
    epart = jnp.zeros((SEQ, E), F32)
    shifts = [None] * CH
    for j in range(CH):
        cols = slice(j * CW, (j + 1) * CW)
        update = dot(mix0, wob[0, :, cols]) + dot(mix1, wob[1, :, cols])
        part = (x1[c, :, cols].astype(F32) + update).astype(BF)
        sb[j] = part
        if j < FIRST:
            shifts[j] = start(STATE + j, sb.at[j], x2.at[c, j], after)
        epart = epart + dot(part, we[cols, :])
    es[0] = epart[:PART].astype(BF)
    es[1] = epart[PART:].astype(BF)
    send_e = start(EPART, es.at[o], er, pair)
    wes[0] = dot(wob[0], we[...]).astype(BF)
    wes[1] = dot(wob[1], we[...]).astype(BF)
    send_e.wait_recv()
    row_ids = c * PART + lax.broadcasted_iota(jnp.int32, (PART, E), 0)
    mine = es[c].astype(F32) + er[...].astype(F32)
    e1s[...] = jnp.where(row_ids < lens[0, s], mine, 0.0).astype(BF)
    ship = start(ESHIP, e1s, e1.at[c], after)
    for j in range(FIRST, CH):
        shifts[j] = start(STATE + j, sb.at[j], x2.at[c, j], after)
    send_we = start(WPART, wes, wer, pair)

    qkv = jnp.zeros((SEQ, 3 * HD), F32)
    total_sq = jnp.zeros((SEQ, 1), F32)
    relays = []
    gather_e, gather_a = {}, {}
    for j in range(CH):
        if j == FIRST:
            ship.wait_recv()
            e_pair = start(EPAIR, e1.at[c], e1.at[c], pair)
            for d, device in peers.items():
                gather_e[d] = start(EGAT + d, e1.at[c], eg.at[d], device)
        rows = slice(j * CW, (j + 1) * CW)
        shifts[j].wait_recv()
        relays.append(start(RELAY + j, x2.at[c, j], x2.at[c, j], pair))
        part = x2[c, j]
        qkv = qkv + dot(part, w[c, rows, :])
        total_sq = total_sq + squares(part)
    e_cross = start(ECROSS, e1.at[c], xe1.at[c], across)
    for j in range(CH):
        relays[j].wait_recv()
        part = x2[o, j]
        qkv = qkv + dot(part, w[o, j * CW : (j + 1) * CW, :])
        total_sq = total_sq + squares(part)
    live = lens[0, prv]
    mixed = attend(qkv, total_sq, live)
    mixed_rows = lax.broadcasted_iota(jnp.int32, (SEQ, HD), 0)
    mx[1, c] = jnp.where(mixed_rows < live, mixed.astype(F32), 0.0).astype(BF)
    send = start(MIX + 1, mx.at[1, c], mx.at[1, c], pair)
    send.wait_recv()
    own_rows = pl.ds(pl.multiple_of(c * PART, PART), PART)
    for d, device in peers.items():
        gather_a[d] = start(AGAT + d, mx.at[1, :, own_rows, :], ag.at[d], device)
    a_cross = start(ACROSS, mx.at[1], xmx, across)

    send_we.wait_recv()
    full = jnp.concatenate(
        [(wes[h].astype(F32) + wer[h].astype(F32)).astype(BF) for h in range(2)], axis=0
    )

    def embed(first, heads):
        heads = jnp.concatenate([heads[0], heads[1]], axis=1)
        return (first.astype(F32) + dot(heads, full)).astype(BF)

    e_pair.wait_recv()
    own = embed(e1[...].reshape(SEQ, E), mx[1])
    e_cross.wait_recv()
    ex_pair = start(EXPAIR, xe1.at[c], xe1.at[c], pair)
    a_cross.wait_recv()
    ex_pair.wait_recv()
    partner = embed(xe1[...].reshape(SEQ, E), xmx[...])
    both = jnp.concatenate([partner, own], axis=0)

    def pieces(slots):
        firsts = jnp.concatenate([e1[c] if d == 0 else eg[d] for d in slots], axis=0)
        heads = [
            jnp.concatenate(
                [mx[1, h, own_rows, :] if d == 0 else ag[d, h] for d in slots], axis=0
            )
            for h in range(2)
        ]
        return embed(firsts, heads)

    total = None
    for slots in ((0, 1, 7, 2), (6, 3, 5, 4)):
        for d in slots:
            if d:
                gather_e[d].wait_recv()
                gather_a[d].wait_recv()
        rows = pieces(slots)
        gram = dot_nt(both, rows).astype(BF)
        for n in range(4):
            h, m = n % 2, n // 2
            term = dot(gram[m * SEQ : (m + 1) * SEQ], rows[:, h * EH : (h + 1) * EH])
            if slots[0] == 0:
                acc[m, h] = term
            else:
                acc[m, h] = acc[m, h] + term
    partner_sum = start(PARTNER, acc.at[0, o], got.at[0], pair)
    own_sum = start(OWN, acc.at[1, o], got.at[1], pair)
    partner_sum.wait_recv()
    back[...] = (acc[0, c] + got[0]).astype(BF)
    give_back = start(BACK, back, gotb, across)
    own_sum.wait_recv()
    acc[1, c] = acc[1, c] + got[1]
    half = jnp.where(c == 0, own[:, :EH].astype(F32), own[:, EH:].astype(F32))
    give_back.wait_recv()
    out[0] = acc[1, c] + gotb[...].astype(F32) - half * float(SEQ * GROUPS)
    for send in sends:
        send.wait_send()


def shards(tokens, lengths, w_query, w_key, w_value, w_out, w_embed):
    anywhere = pl.BlockSpec(memory_space=pl.ANY)
    total = pl.pallas_call(
        kernel,
        out_shape=jax.ShapeDtypeStruct((1, SEQ, EH), F32),
        in_specs=[anywhere, pl.BlockSpec(memory_space=pltpu.SMEM)] + [anywhere] * 5,
        out_specs=pl.BlockSpec(memory_space=pltpu.VMEM),
        scratch_shapes=[
            pltpu.VMEM((2, SEQ, HALF), BF),
            pltpu.VMEM((2, HALF, 3 * HD), BF),
            pltpu.VMEM((2, HD, HALF), BF),
            pltpu.VMEM((HALF, E), BF),
            pltpu.VMEM((CH, SEQ, CW), BF),
            pltpu.VMEM((2, CH, SEQ, CW), BF),
            pltpu.VMEM((2, 2, SEQ, HD), BF),
            pltpu.VMEM((2, PART, E), BF),
            pltpu.VMEM((PART, E), BF),
            pltpu.VMEM((PART, E), BF),
            pltpu.VMEM((2, PART, E), BF),
            pltpu.VMEM((2, PART, E), BF),
            pltpu.VMEM((8, PART, E), BF),
            pltpu.VMEM((8, 2, PART, HD), BF),
            pltpu.VMEM((2, SEQ, HD), BF),
            pltpu.VMEM((2, HD, E), BF),
            pltpu.VMEM((2, HD, E), BF),
            pltpu.VMEM((2, 2, SEQ, EH), F32),
            pltpu.VMEM((2, SEQ, EH), F32),
            pltpu.VMEM((SEQ, EH), BF),
            pltpu.VMEM((SEQ, EH), BF),
            pltpu.SemaphoreType.DMA((9,)),
            pltpu.SemaphoreType.DMA((REMOTES,)),
            pltpu.SemaphoreType.DMA((REMOTES,)),
        ],
        compiler_params=pltpu.CompilerParams(
            collective_id=0, has_side_effects=True, vmem_limit_bytes=60 * 1024 * 1024
        ),
    )(tokens, lengths.reshape(1, SECTIONS), w_query, w_key, w_value, w_out, w_embed)
    return total * (1.0 / (SEQ * GROUPS))


def solution(mesh):
    return jax.shard_map(
        shards,
        mesh=mesh,
        in_specs=(
            P("section", "dp", "tensor"),
            P(None, "dp"),
            P("section", None, "tensor"),
            P("section", None, "tensor"),
            P("section", None, "tensor"),
            P("section", "tensor", None),
            P("tensor", None),
        ),
        out_specs=P("section", "dp", "tensor"),
        check_vma=False,
    )
```

time: 79.8 us -> 81.5 us (1.021)
  local copies, waits for them, and re-layouts: 3.01 us -> 0 us
  Pallas kernels: 76.5 us -> 79.3 us
  other arithmetic: 0 us -> 1.67 us
    unnamed x2 -> x0, local copies, waits for them, and re-layouts: 3.01 us -> none
    pallas_call x1, Pallas kernels: 76.5 us -> 79.3 us  [shards(): pl.pallas_call(kernel, out_shape=jax.ShapeDtypeStruct((1, SEQ, EH), F32),...]
    mul x0 -> x1, other arithmetic: none -> 1.67 us  [shards(): return total * (1.0 / (SEQ * GROUPS))]
where the time goes in v3:
time: 81.5 us; the launch traced here: 81 us
  Pallas kernels  79.3 us (97%)
  other arithmetic  1.67 us (2%)
    pallas_call x1, Pallas kernels, shards(): pl.pallas_call(kernel, out_shape=jax.ShapeDtypeStruct((1, SEQ, EH), F32),...  79.3 us
    mul x1, other arithmetic, shards(): return total * (1.0 / (SEQ * GROUPS))  1.67 us

profile of v3, /device:TPU:1, one launch (start us, length us, event | category | flops | bytes accessed | tf_op | source)
XLA Modules:
  0.0 81.0 jit_solution(8579625065869906269)
XLA Ops:
  0.0 79.3 %shard_map.73 = f32[1,128,512]{2,1,0:T(8,128)} custom-call(bf16[1,128,2048]{2,1,0:T(8,128)(2,1)} %tok.1, s32[1,32]{1,0:T(1,128)} %bitcast.1, bf16[1,4096,128]{2,1,0:T(8,128)(2,1)} %wq.1, bf16[1,4096,128]{2,1,0:T(8,128)(2,1)} %wk.1, bf16[1,4096,128]{2,1,0:T(8,128)(2,1)} %wv.1, bf16[1,128,4096]{2,1,0:T(8,128)(2,1)} %wo.1, bf16[2048,1024]{1,0:T(8,128)(2,1)} %wemb.1), custom_call_target="tpu_custom_call" | custom-call | tf_op jit(solution)/shard_map/pallas_call | solution.py:257
  79.3 1.7 %broadcast_multiply_fusion = f32[1,128,512]{2,1,0:T(8,128)} fusion(f32[1,128,512]{2,1,0:T(8,128)} %shard_map.73), kind=kLoop, calls=%fused_computation | loop fusion | flops 65536 | bytes 524288 | tf_op jit(solution)/shard_map/mul | solution.py:292

commit v4 on v3

--- a/solution.py
+++ b/solution.py
@@ -22,7 +22,7 @@
 BF = jnp.bfloat16
 F32 = jnp.float32
 
-FIRST = 3
+FIRST = 2
 (TOK, WOUT, MIX, EPART, WPART, ESHIP, EPAIR, ECROSS, EXPAIR, ACROSS, PARTNER, OWN, BACK) = (
     0, 1, 2, 4, 5, 6, 7, 8, 9, 10, 11, 12, 13)
 STATE = 14
@@ -136,9 +136,7 @@
         sends.append(copy)
         return copy
 
-    loads[8].wait()
     mix0, mix1 = mx[0, 0], mx[0, 1]
-    epart = jnp.zeros((SEQ, E), F32)
     shifts = [None] * CH
     for j in range(CH):
         cols = slice(j * CW, (j + 1) * CW)
@@ -147,12 +145,11 @@
         sb[j] = part
         if j < FIRST:
             shifts[j] = start(STATE + j, sb.at[j], x2.at[c, j], after)
-        epart = epart + dot(part, we[cols, :])
+    loads[8].wait()
+    epart = dot(jnp.concatenate([sb[j] for j in range(CH)], axis=1), we[...])
     es[0] = epart[:PART].astype(BF)
     es[1] = epart[PART:].astype(BF)
     send_e = start(EPART, es.at[o], er, pair)
-    wes[0] = dot(wob[0], we[...]).astype(BF)
-    wes[1] = dot(wob[1], we[...]).astype(BF)
     send_e.wait_recv()
     row_ids = c * PART + lax.broadcasted_iota(jnp.int32, (PART, E), 0)
     mine = es[c].astype(F32) + er[...].astype(F32)
@@ -160,6 +157,8 @@
     ship = start(ESHIP, e1s, e1.at[c], after)
     for j in range(FIRST, CH):
         shifts[j] = start(STATE + j, sb.at[j], x2.at[c, j], after)
+    wes[0] = dot(wob[0], we[...]).astype(BF)
+    wes[1] = dot(wob[1], we[...]).astype(BF)
     send_we = start(WPART, wes, wer, pair)
 
     qkv = jnp.zeros((SEQ, 3 * HD), F32)

time: 81.5 us -> 81.6 us (level)
  no operation moved by 1% of the time
where the time goes in v4:
time: 81.6 us; the launch traced here: 80.7 us
  Pallas kernels  79 us (97%)
  other arithmetic  1.67 us (2%)
    pallas_call x1, Pallas kernels, shards(): pl.pallas_call(kernel, out_shape=jax.ShapeDtypeStruct((1, SEQ, EH), F32),...  79 us
    mul x1, other arithmetic, shards(): return total * (1.0 / (SEQ * GROUPS))  1.67 us

profile of v4, /device:TPU:1, one launch (start us, length us, event | category | flops | bytes accessed | tf_op | source)
XLA Modules:
  0.0 80.7 jit_solution(5879817164530199409)
XLA Ops:
  0.0 79.0 %shard_map.73 = f32[1,128,512]{2,1,0:T(8,128)} custom-call(bf16[1,128,2048]{2,1,0:T(8,128)(2,1)} %tok.1, s32[1,32]{1,0:T(1,128)} %bitcast.1, bf16[1,4096,128]{2,1,0:T(8,128)(2,1)} %wq.1, bf16[1,4096,128]{2,1,0:T(8,128)(2,1)} %wk.1, bf16[1,4096,128]{2,1,0:T(8,128)(2,1)} %wv.1, bf16[1,128,4096]{2,1,0:T(8,128)(2,1)} %wo.1, bf16[2048,1024]{1,0:T(8,128)(2,1)} %wemb.1), custom_call_target="tpu_custom_call" | custom-call | tf_op jit(solution)/shard_map/pallas_call | solution.py:256
  79.0 1.7 %broadcast_multiply_fusion = f32[1,128,512]{2,1,0:T(8,128)} fusion(f32[1,128,512]{2,1,0:T(8,128)} %shard_map.73), kind=kLoop, calls=%fused_computation | loop fusion | flops 65536 | bytes 524288 | tf_op jit(solution)/shard_map/mul | solution.py:291

commit v5 on v4

--- a/solution.py
+++ b/solution.py
@@ -28,7 +28,7 @@
 STATE = 14
 RELAY = STATE + CH
 EGAT = RELAY + CH
-AGAT = EGAT + 8
+AGAT = EGAT + 16
 REMOTES = AGAT + 8
 
 
@@ -165,12 +165,29 @@
     total_sq = jnp.zeros((SEQ, 1), F32)
     relays = []
     gather_e, gather_a = {}, {}
+
+    def ring(q, src, target, device):
+        gather_e[target, q] = start(EGAT + 2 * target + q, src, eg.at[target, q], device)
+
+    def take(slot):
+        for q in range(2):
+            gather_e[slot, q].wait_recv()
+            if slot < 3 or (slot == 3 and q == 0):
+                ring(q, eg.at[slot, q], slot + 1, peers[1])
+            if slot > 5 or (slot == 5 and q == 1):
+                ring(q, eg.at[slot, q], slot - 1, peers[7])
+
     for j in range(CH):
         if j == FIRST:
             ship.wait_recv()
             e_pair = start(EPAIR, e1.at[c], e1.at[c], pair)
-            for d, device in peers.items():
-                gather_e[d] = start(EGAT + d, e1.at[c], eg.at[d], device)
+            for q in range(2):
+                src = e1.at[c, q * 32 : (q + 1) * 32, :]
+                ring(q, src, 1, peers[1])
+                ring(q, src, 7, peers[7])
+        if j == 6:
+            take(1)
+            take(7)
         rows = slice(j * CW, (j + 1) * CW)
         shifts[j].wait_recv()
         relays.append(start(RELAY + j, x2.at[c, j], x2.at[c, j], pair))
@@ -188,6 +205,8 @@
     mixed_rows = lax.broadcasted_iota(jnp.int32, (SEQ, HD), 0)
     mx[1, c] = jnp.where(mixed_rows < live, mixed.astype(F32), 0.0).astype(BF)
     send = start(MIX + 1, mx.at[1, c], mx.at[1, c], pair)
+    take(2)
+    take(6)
     send.wait_recv()
     own_rows = pl.ds(pl.multiple_of(c * PART, PART), PART)
     for d, device in peers.items():
@@ -205,6 +224,8 @@
 
     e_pair.wait_recv()
     own = embed(e1[...].reshape(SEQ, E), mx[1])
+    take(3)
+    take(5)
     e_cross.wait_recv()
     ex_pair = start(EXPAIR, xe1.at[c], xe1.at[c], pair)
     a_cross.wait_recv()
@@ -213,7 +234,7 @@
     both = jnp.concatenate([partner, own], axis=0)
 
     def pieces(slots):
-        firsts = jnp.concatenate([e1[c] if d == 0 else eg[d] for d in slots], axis=0)
+        firsts = jnp.concatenate([e1[c] if d == 0 else eg[d].reshape(PART, E) for d in slots], axis=0)
         heads = [
             jnp.concatenate(
                 [mx[1, h, own_rows, :] if d == 0 else ag[d, h] for d in slots], axis=0
@@ -222,11 +243,11 @@
         ]
         return embed(firsts, heads)
 
-    total = None
     for slots in ((0, 1, 7, 2), (6, 3, 5, 4)):
         for d in slots:
+            if d == 4:
+                take(4)
             if d:
-                gather_e[d].wait_recv()
                 gather_a[d].wait_recv()
         rows = pieces(slots)
         gram = dot_nt(both, rows).astype(BF)
@@ -271,7 +292,7 @@
             pltpu.VMEM((PART, E), BF),
             pltpu.VMEM((2, PART, E), BF),
             pltpu.VMEM((2, PART, E), BF),
-            pltpu.VMEM((8, PART, E), BF),
+            pltpu.VMEM((8, 2, PART // 2, E), BF),
             pltpu.VMEM((8, 2, PART, HD), BF),
             pltpu.VMEM((2, SEQ, HD), BF),
             pltpu.VMEM((2, HD, E), BF),

time: 81.6 us -> 72.8 us (0.89)
  Pallas kernels: 79 us -> 70 us
    pallas_call x1, Pallas kernels: 79 us -> 70 us  [shards(): pl.pallas_call(kernel, out_shape=jax.ShapeDtypeStruct((1, SEQ, EH), F32),...]
where the time goes in v5:
time: 72.8 us; the launch traced here: 71.7 us
  Pallas kernels  70 us (96%)
  other arithmetic  1.67 us (2%)
    pallas_call x1, Pallas kernels, shards(): pl.pallas_call(kernel, out_shape=jax.ShapeDtypeStruct((1, SEQ, EH), F32),...  70 us
    mul x1, other arithmetic, shards(): return total * (1.0 / (SEQ * GROUPS))  1.67 us

profile of v5, /device:TPU:1, one launch (start us, length us, event | category | flops | bytes accessed | tf_op | source)
XLA Modules:
  0.0 71.7 jit_solution(5237637102015929822)
XLA Ops:
  0.0 70.0 %shard_map.73 = f32[1,128,512]{2,1,0:T(8,128)} custom-call(bf16[1,128,2048]{2,1,0:T(8,128)(2,1)} %tok.1, s32[1,32]{1,0:T(1,128)} %bitcast.1, bf16[1,4096,128]{2,1,0:T(8,128)(2,1)} %wq.1, bf16[1,4096,128]{2,1,0:T(8,128)(2,1)} %wk.1, bf16[1,4096,128]{2,1,0:T(8,128)(2,1)} %wv.1, bf16[1,128,4096]{2,1,0:T(8,128)(2,1)} %wo.1, bf16[2048,1024]{1,0:T(8,128)(2,1)} %wemb.1), custom_call_target="tpu_custom_call" | custom-call | tf_op jit(solution)/shard_map/pallas_call | solution.py:277
  70.0 1.7 %broadcast_multiply_fusion = f32[1,128,512]{2,1,0:T(8,128)} fusion(f32[1,128,512]{2,1,0:T(8,128)} %shard_map.73), kind=kLoop, calls=%fused_computation | loop fusion | flops 65536 | bytes 524288 | tf_op jit(solution)/shard_map/mul | solution.py:312

commit v6 on v5

--- a/solution.py
+++ b/solution.py
@@ -23,9 +23,9 @@
 F32 = jnp.float32
 
 FIRST = 2
-(TOK, WOUT, MIX, EPART, WPART, ESHIP, EPAIR, ECROSS, EXPAIR, ACROSS, PARTNER, OWN, BACK) = (
-    0, 1, 2, 4, 5, 6, 7, 8, 9, 10, 11, 12, 13)
-STATE = 14
+(TOK, WOUT, MIX, EPART, WPART, ESHIP, EPAIR, ECROSS, EXPAIR, ACROSS, OWN, PARTNER, BACK) = (
+    0, 1, 2, 4, 5, 6, 7, 8, 9, 10, 11, 12, 14)
+STATE = 16
 RELAY = STATE + CH
 EGAT = RELAY + CH
 AGAT = EGAT + 16
@@ -185,7 +185,7 @@
                 src = e1.at[c, q * 32 : (q + 1) * 32, :]
                 ring(q, src, 1, peers[1])
                 ring(q, src, 7, peers[7])
-        if j == 6:
+        if j == 5:
             take(1)
             take(7)
         rows = slice(j * CW, (j + 1) * CW)
@@ -195,6 +195,8 @@
         qkv = qkv + dot(part, w[c, rows, :])
         total_sq = total_sq + squares(part)
     e_cross = start(ECROSS, e1.at[c], xe1.at[c], across)
+    take(2)
+    take(6)
     for j in range(CH):
         relays[j].wait_recv()
         part = x2[o, j]
@@ -205,8 +207,6 @@
     mixed_rows = lax.broadcasted_iota(jnp.int32, (SEQ, HD), 0)
     mx[1, c] = jnp.where(mixed_rows < live, mixed.astype(F32), 0.0).astype(BF)
     send = start(MIX + 1, mx.at[1, c], mx.at[1, c], pair)
-    take(2)
-    take(6)
     send.wait_recv()
     own_rows = pl.ds(pl.multiple_of(c * PART, PART), PART)
     for d, device in peers.items():
@@ -251,22 +251,35 @@
                 gather_a[d].wait_recv()
         rows = pieces(slots)
         gram = dot_nt(both, rows).astype(BF)
-        for n in range(4):
-            h, m = n % 2, n // 2
-            term = dot(gram[m * SEQ : (m + 1) * SEQ], rows[:, h * EH : (h + 1) * EH])
-            if slots[0] == 0:
-                acc[m, h] = term
-            else:
-                acc[m, h] = acc[m, h] + term
-    partner_sum = start(PARTNER, acc.at[0, o], got.at[0], pair)
+        if slots[0] == 0:
+            for m in range(2):
+                for h in range(2):
+                    acc[m, h] = dot(gram[m * SEQ : (m + 1) * SEQ], rows[:, h * EH : (h + 1) * EH])
+    partner_sum = []
+    for m in range(2):
+        part_rows = slice(m * PART, (m + 1) * PART)
+        for h in range(2):
+            term = dot(gram[part_rows], rows[:, h * EH : (h + 1) * EH])
+            acc[0, h, part_rows, :] = acc[0, h, part_rows, :] + term
+        partner_sum.append(
+            start(PARTNER + m, acc.at[0, o, part_rows, :], got.at[0, part_rows, :], pair)
+        )
+    for h in range(2):
+        acc[1, h] = acc[1, h] + dot(gram[SEQ:], rows[:, h * EH : (h + 1) * EH])
     own_sum = start(OWN, acc.at[1, o], got.at[1], pair)
-    partner_sum.wait_recv()
-    back[...] = (acc[0, c] + got[0]).astype(BF)
-    give_back = start(BACK, back, gotb, across)
+    give_back = []
+    for m in range(2):
+        part_rows = slice(m * PART, (m + 1) * PART)
+        partner_sum[m].wait_recv()
+        back[part_rows, :] = (acc[0, c, part_rows, :] + got[0, part_rows, :]).astype(BF)
+        give_back.append(
+            start(BACK + m, back.at[part_rows, :], gotb.at[part_rows, :], across)
+        )
     own_sum.wait_recv()
     acc[1, c] = acc[1, c] + got[1]
     half = jnp.where(c == 0, own[:, :EH].astype(F32), own[:, EH:].astype(F32))
-    give_back.wait_recv()
+    for copy in give_back:
+        copy.wait_recv()
     out[0] = acc[1, c] + gotb[...].astype(F32) - half * float(SEQ * GROUPS)
     for send in sends:
         send.wait_send()

time: 72.8 us -> 71.6 us (0.984); the launches traced: 71.7 us -> 71.4 us
  no operation moved by 1% of the time
where the time goes in v6:
time: 71.6 us; the launch traced here: 71.4 us
  Pallas kernels  69.8 us (97%)
  other arithmetic  1.67 us (2%)
    pallas_call x1, Pallas kernels, shards(): pl.pallas_call(kernel, out_shape=jax.ShapeDtypeStruct((1, SEQ, EH), F32),...  69.8 us
    mul x1, other arithmetic, shards(): return total * (1.0 / (SEQ * GROUPS))  1.67 us

profile of v6, /device:TPU:1, one launch (start us, length us, event | category | flops | bytes accessed | tf_op | source)
XLA Modules:
  0.0 71.4 jit_solution(9688399428085355860)
XLA Ops:
  0.0 69.8 %shard_map.73 = f32[1,128,512]{2,1,0:T(8,128)} custom-call(bf16[1,128,2048]{2,1,0:T(8,128)(2,1)} %tok.1, s32[1,32]{1,0:T(1,128)} %bitcast.1, bf16[1,4096,128]{2,1,0:T(8,128)(2,1)} %wq.1, bf16[1,4096,128]{2,1,0:T(8,128)(2,1)} %wk.1, bf16[1,4096,128]{2,1,0:T(8,128)(2,1)} %wv.1, bf16[1,128,4096]{2,1,0:T(8,128)(2,1)} %wo.1, bf16[2048,1024]{1,0:T(8,128)(2,1)} %wemb.1), custom_call_target="tpu_custom_call" | custom-call | tf_op jit(solution)/shard_map/pallas_call | solution.py:290
  69.8 1.7 %broadcast_multiply_fusion = f32[1,128,512]{2,1,0:T(8,128)} fusion(f32[1,128,512]{2,1,0:T(8,128)} %shard_map.73), kind=kLoop, calls=%fused_computation | loop fusion | flops 65536 | bytes 524288 | tf_op jit(solution)/shard_map/mul | solution.py:325

commit v7 on v6

--- a/solution.py
+++ b/solution.py
@@ -29,7 +29,8 @@
 RELAY = STATE + CH
 EGAT = RELAY + CH
 AGAT = EGAT + 16
-REMOTES = AGAT + 8
+ACAT = AGAT + 16
+REMOTES = ACAT + 2
 
 
 def dot(a, b):
@@ -75,13 +76,15 @@
     before = (prv, g, c)
     across = (s, y * 2 + 1 - xh, c)
     peers = {d: (s, lax.rem(y + d, 8) * 2 + xh, c) for d in (4, 3, 5, 2, 6, 1, 7)}
+    facing = [(s, across[1], k) for k in range(2)]
+    others = [(s, device[1], k) for device in peers.values() for k in range(2)]
 
     def local(i, src, dst):
         return pltpu.make_async_copy(src, dst, lsem.at[i])
 
-    def remote(i, src, dst, device):
+    def remote(i, src, dst, device, landed=None):
         return pltpu.make_async_remote_copy(
-            src_ref=src, dst_ref=dst, send_sem=ssem.at[i], recv_sem=rsem.at[i],
+            src_ref=src, dst_ref=dst, send_sem=ssem.at[i], recv_sem=rsem.at[i if landed is None else landed],
             device_id=device, device_id_type=pl.DeviceIdType.MESH,
         )
 
@@ -99,9 +102,9 @@
         copy.start()
 
     barrier = pltpu.get_barrier_semaphore()
-    for device in (pair, after, before, across, *peers.values()):
+    for device in (pair, after, before, *facing, *others):
         pl.semaphore_signal(barrier, inc=1, device_id=device, device_id_type=pl.DeviceIdType.MESH)
-    pl.semaphore_wait(barrier, 11)
+    pl.semaphore_wait(barrier, 19)
 
     send_tok = remote(TOK, tok.at[0], x1.at[c], pair)
     send_tok.start()
@@ -130,8 +133,8 @@
     send_wo.wait_recv()
     send.wait_recv()
 
-    def start(i, src, dst, device):
-        copy = remote(i, src, dst, device)
+    def start(i, src, dst, device, landed=None):
+        copy = remote(i, src, dst, device, landed)
         copy.start()
         sends.append(copy)
         return copy
@@ -164,7 +167,7 @@
     qkv = jnp.zeros((SEQ, 3 * HD), F32)
     total_sq = jnp.zeros((SEQ, 1), F32)
     relays = []
-    gather_e, gather_a = {}, {}
+    gather_e = {}
 
     def ring(q, src, target, device):
         gather_e[target, q] = start(EGAT + 2 * target + q, src, eg.at[target, q], device)
@@ -207,11 +210,15 @@
     mixed_rows = lax.broadcasted_iota(jnp.int32, (SEQ, HD), 0)
     mx[1, c] = jnp.where(mixed_rows < live, mixed.astype(F32), 0.0).astype(BF)
     send = start(MIX + 1, mx.at[1, c], mx.at[1, c], pair)
-    send.wait_recv()
+    for d, device in peers.items():
+        for k in range(2):
+            start(
+                AGAT + 2 * d + k, mx.at[1, c, k * PART : (k + 1) * PART, :], ag.at[d, c],
+                (s, device[1], k), AGAT + 2 * d + c,
+            )
+    for k in range(2):
+        start(ACAT + k, mx.at[1, c], xmx.at[c], facing[k], ACAT + c)
     own_rows = pl.ds(pl.multiple_of(c * PART, PART), PART)
-    for d, device in peers.items():
-        gather_a[d] = start(AGAT + d, mx.at[1, :, own_rows, :], ag.at[d], device)
-    a_cross = start(ACROSS, mx.at[1], xmx, across)
 
     send_we.wait_recv()
     full = jnp.concatenate(
@@ -223,12 +230,14 @@
         return (first.astype(F32) + dot(heads, full)).astype(BF)
 
     e_pair.wait_recv()
+    send.wait_recv()
     own = embed(e1[...].reshape(SEQ, E), mx[1])
     take(3)
     take(5)
     e_cross.wait_recv()
     ex_pair = start(EXPAIR, xe1.at[c], xe1.at[c], pair)
-    a_cross.wait_recv()
+    for h in range(2):
+        remote(ACAT + h, xmx.at[h], xmx.at[h], across).wait_recv()
     ex_pair.wait_recv()
     partner = embed(xe1[...].reshape(SEQ, E), xmx[...])
     both = jnp.concatenate([partner, own], axis=0)
@@ -248,7 +257,8 @@
             if d == 4:
                 take(4)
             if d:
-                gather_a[d].wait_recv()
+                for h in range(2):
+                    remote(AGAT + 2 * d + h, ag.at[d, h], ag.at[d, h], across).wait_recv()
         rows = pieces(slots)
         gram = dot_nt(both, rows).astype(BF)
         if slots[0] == 0:

time: 71.6 us -> 70.9 us (level)
  Pallas kernels: 69.8 us -> 68.6 us
    pallas_call x1, Pallas kernels: 69.8 us -> 68.6 us  [shards(): pl.pallas_call(kernel, out_shape=jax.ShapeDtypeStruct((1, SEQ, EH), F32),...]
where the time goes in v7:
time: 70.9 us; the launch traced here: 70.3 us
  Pallas kernels  68.6 us (97%)
  other arithmetic  1.67 us (2%)
    pallas_call x1, Pallas kernels, shards(): pl.pallas_call(kernel, out_shape=jax.ShapeDtypeStruct((1, SEQ, EH), F32),...  68.6 us
    mul x1, other arithmetic, shards(): return total * (1.0 / (SEQ * GROUPS))  1.67 us

profile of v7, /device:TPU:1, one launch (start us, length us, event | category | flops | bytes accessed | tf_op | source)
XLA Modules:
  0.0 70.3 jit_solution(13533633691650042491)
XLA Ops:
  0.0 68.6 %shard_map.73 = f32[1,128,512]{2,1,0:T(8,128)} custom-call(bf16[1,128,2048]{2,1,0:T(8,128)(2,1)} %tok.1, s32[1,32]{1,0:T(1,128)} %bitcast.1, bf16[1,4096,128]{2,1,0:T(8,128)(2,1)} %wq.1, bf16[1,4096,128]{2,1,0:T(8,128)(2,1)} %wk.1, bf16[1,4096,128]{2,1,0:T(8,128)(2,1)} %wv.1, bf16[1,128,4096]{2,1,0:T(8,128)(2,1)} %wo.1, bf16[2048,1024]{1,0:T(8,128)(2,1)} %wemb.1), custom_call_target="tpu_custom_call" | custom-call | tf_op jit(solution)/shard_map/pallas_call | solution.py:300
  68.6 1.7 %broadcast_multiply_fusion = f32[1,128,512]{2,1,0:T(8,128)} fusion(f32[1,128,512]{2,1,0:T(8,128)} %shard_map.73), kind=kLoop, calls=%fused_computation | loop fusion | flops 65536 | bytes 524288 | tf_op jit(solution)/shard_map/mul | solution.py:335
